TPU v7x, 32 devices: a whole 2x2x4 slice. The times are simulated.
32 devices in a mesh: drive: 2 (over y), tm: 4 (over z), mom: 2 (over x), col: 2 (over core).
Axes of the slice: x: 2, y: 2, z: 4, core: 2. Of those that a mesh axis runs over, the one named last changes fastest.
Arguments:
- propagators: float32 [8, 8, 384, 384], P(('drive', 'mom'), 'tm', None, 'col'), parts along dimension 0, as said below
- current_op: float32 [4, 384, 384], P('mom'), may hold values from -6 to 6
Outputs:
- spectrum: float32 [8, 2, 8, 384, 384], P(('drive', 'mom'), None, None, 'tm', 'col'), parts along dimension 0
There are 2 independent parts, one for each index of `drive`. A program takes and returns all parts, laid end to end along the dimension named above; an argument that names none is the same for every part. Nothing has to cross between parts.
Inputs may be any that keep to these rules, and one draw needn't show every extreme that they name: Every matrix propagators[k, t] is orthogonal to float32 rounding, with dense entries.
All inputs are finite; a program needn't handle non-finite values.
Results may differ from a plain program's by a relative error of at most 0.0003.
Values sent between devices are 32-bit elements; how exact they have to be, the bound alone decides.
No kernel may reach another device: no remote copies, remote signals or barrier semaphores. Data moves between devices by JAX's collectives and lax.ppermute only.
A program may use at most 64 MiB of HBM per device.

v0:
```python
import math

import jax
import jax.numpy as jnp
from jax import lax
from jax.sharding import PartitionSpec as P


def prefix_2(value, axis, join, neutral):
    count, mine = (lax.axis_size(axis), lax.axis_index(axis))
    pieces = lax.all_gather(value, axis)
    running = jnp.full_like(value, 0) + jnp.asarray(neutral, value.dtype)

    def turn(position, running):
        longer = join(running, pieces[position])
        return jnp.where(position < mine, longer, running)

    return lax.fori_loop(0, count - 1, turn, running)


def multiply(left, right):
    return jnp.einsum("kab,kbc->kac", left, right, precision=lax.Precision.HIGHEST)


def later_first(earlier, later):
    return multiply(later, earlier)


def chain_step(carry, unit):
    nxt = multiply(unit, carry)
    return (nxt, nxt)


def spectrum_block(block):
    length = block.shape[1]
    freq = lax.broadcasted_iota(jnp.int32, (length, length), 0)
    times = lax.broadcasted_iota(jnp.int32, (length, length), 1)
    phase = 2.0 * math.pi / length * (freq * times % length).astype(jnp.float32)
    scale = 1.0 / math.sqrt(length)
    cosine = jnp.cos(phase) * scale
    sine = -jnp.sin(phase) * scale
    real = jnp.einsum("ft,ktrc->kfrc", cosine, block, precision=lax.Precision.HIGHEST)
    imag = jnp.einsum("ft,ktrc->kfrc", sine, block, precision=lax.Precision.HIGHEST)
    return jnp.stack([real, imag], axis=1)


def owner_block(block):
    return spectrum_block(block[:, :, 0])


def body(propagators, current_op):
    sym = 0.5 * (current_op + jnp.swapaxes(current_op, 1, 2))
    whole = lax.all_to_all(propagators, "col", split_axis=1, concat_axis=3, tiled=True)
    kdev = whole.shape[0]
    order = whole.shape[2]
    units = jnp.moveaxis(whole, 1, 0)
    total = units[0]
    identity = jnp.broadcast_to(jnp.eye(order, dtype=jnp.float32), total.shape)
    carry_in = prefix_2(total, ("tm", "col"), later_first, identity)
    _, applied = lax.scan(chain_step, carry_in, units)
    prefix = jnp.moveaxis(applied, 0, 1)
    weighted = jnp.einsum("kab,ksbc->ksac", sym, prefix, precision=lax.Precision.HIGHEST)
    n_rows = lax.axis_size("tm")
    n_cols = lax.axis_size("col")
    row_width = order // n_rows
    col_width = order // n_cols
    slices = prefix.shape[1]
    left = prefix.reshape(kdev, slices, order, n_rows, row_width)
    right = weighted.reshape(kdev, slices, order, n_cols, col_width)
    heis = jnp.einsum("ksbir,ksbjq->ksijrq", left, right, precision=lax.Precision.HIGHEST)
    heis = heis.reshape(kdev, slices, n_rows * n_cols, row_width, col_width)
    return owner_block(lax.all_to_all(heis, ("tm", "col"), split_axis=2, concat_axis=1, tiled=True))


def solution(mesh):
    return jax.shard_map(
        body,
        mesh=mesh,
        in_specs=(P(("drive", "mom"), "tm", None, "col"), P("mom", None, None)),
        out_specs=P(("drive", "mom"), None, None, "tm", "col"),
        check_vma=False,
    )
```

profile of v0, /device:TPU:0, one launch (start us, length us, event | category | flops | bytes accessed | tf_op | source)
XLA Modules:
  0.0 198.6 jit_solution(8359196111122669494)
XLA Ops:
  6.5 1.3 copy.15
  7.9 4.7 %all_to_all.24 = f32[2,2,384,192]{2,3,0,1:T(8,128)S(1)} all-to-all(f32[2,2,384,192]{2,3,0,1:T(8,128)S(1)} %copy.15), channel_id=1, replica_groups=mesh['drive'=2,'tm'=4,'mom'=2,'col'=2] {'col'}, dimensions={1} | all-to-all | bytes 2359296 | tf_op jit(solution)/shard_map/all_to_all | solution.py:53
  12.7 1.4 copy.17
  14.1 1.2 copy-done
  15.3 1.4 copy.20
  16.7 0.9 fusion.19
  17.5 90.1 %all-gather.2.cloned.1.call-done = f32[8,2,384,384]{3,2,1,0:T(8,128)} async-done(((f32[1,2,384,384]{3,2,1,0:T(8,128)}), f32[8,2,384,384]{3,2,1,0:T(8,128)}) %all-gather.2.cloned.1.call-update) | async-done | bytes 9437200 | tf_op jit(solution)/shard_map/all_gather | solution.py:11
  107.7 1.1 broadcast_in_dim.7
  108.8 26.5 %while.8 = (s32[]{:T(128)}, f32[2,384,384]{2,1,0:T(8,128)S(1)}, s32[]{:T(128)}, f32[8,2,384,384]{3,2,1,0:T(8,128)}, s32[]{:T(128)}) while((s32[]{:T(128)}, f32[2,384,384]{2,1,0:T(8,128)S(1)}, s32[]{:T(128)}, f32[8,2,384,384]{3,2,1,0:T(8,128)}, s32[]{:T(128)}) %tuple.31), condition=%wide.region_1.2_spmd, body=%wide.region_0.1_spmd.sunk | while | flops 1359249408 | bytes 7077971 | solution.py:18
  108.8 0.1 copy.48
  108.9 3.7 %convolution_select_fusion.2 = f32[2,384,384]{2,1,0:T(8,128)S(1)} fusion(f32[2,384,384]{2,1,0:T(8,128)S(1)} %copy.48, f32[8,2,384,384]{3,2,1,0:T(8,128)} %get-tuple-element.147, s32[]{:T(128)S(6)} %copy.41, pred[]{:T(512)S(6)} %lt.40), kind=kOutput, calls=%fused_computation.clone.1 | convolution fusion | flops 1359249408 | bytes 4718597 | tf_op jit(solution)/shard_map/while/body/eval_jaxpr/kab,kbc->kac/dot_general | solution.py:22
  112.6 0.1 copy.48
  112.7 3.7 %convolution_select_fusion.2 = f32[2,384,384]{2,1,0:T(8,128)S(1)} fusion(f32[2,384,384]{2,1,0:T(8,128)S(1)} %copy.48, f32[8,2,384,384]{3,2,1,0:T(8,128)} %get-tuple-element.147, s32[]{:T(128)S(6)} %copy.41, pred[]{:T(512)S(6)} %lt.40), kind=kOutput, calls=%fused_computation.clone.1 | convolution fusion | flops 1359249408 | bytes 4718597 | tf_op jit(solution)/shard_map/while/body/eval_jaxpr/kab,kbc->kac/dot_general | solution.py:22
  116.4 0.1 copy.48
  116.5 3.7 %convolution_select_fusion.2 = f32[2,384,384]{2,1,0:T(8,128)S(1)} fusion(f32[2,384,384]{2,1,0:T(8,128)S(1)} %copy.48, f32[8,2,384,384]{3,2,1,0:T(8,128)} %get-tuple-element.147, s32[]{:T(128)S(6)} %copy.41, pred[]{:T(512)S(6)} %lt.40), kind=kOutput, calls=%fused_computation.clone.1 | convolution fusion | flops 1359249408 | bytes 4718597 | tf_op jit(solution)/shard_map/while/body/eval_jaxpr/kab,kbc->kac/dot_general | solution.py:22
  120.2 0.1 copy.48
  120.3 3.7 %convolution_select_fusion.2 = f32[2,384,384]{2,1,0:T(8,128)S(1)} fusion(f32[2,384,384]{2,1,0:T(8,128)S(1)} %copy.48, f32[8,2,384,384]{3,2,1,0:T(8,128)} %get-tuple-element.147, s32[]{:T(128)S(6)} %copy.41, pred[]{:T(512)S(6)} %lt.40), kind=kOutput, calls=%fused_computation.clone.1 | convolution fusion | flops 1359249408 | bytes 4718597 | tf_op jit(solution)/shard_map/while/body/eval_jaxpr/kab,kbc->kac/dot_general | solution.py:22
  124.0 0.1 copy.48
  124.1 3.7 %convolution_select_fusion.2 = f32[2,384,384]{2,1,0:T(8,128)S(1)} fusion(f32[2,384,384]{2,1,0:T(8,128)S(1)} %copy.48, f32[8,2,384,384]{3,2,1,0:T(8,128)} %get-tuple-element.147, s32[]{:T(128)S(6)} %copy.41, pred[]{:T(512)S(6)} %lt.40), kind=kOutput, calls=%fused_computation.clone.1 | convolution fusion | flops 1359249408 | bytes 4718597 | tf_op jit(solution)/shard_map/while/body/eval_jaxpr/kab,kbc->kac/dot_general | solution.py:22
  127.8 0.1 copy.48
  127.8 3.7 %convolution_select_fusion.2 = f32[2,384,384]{2,1,0:T(8,128)S(1)} fusion(f32[2,384,384]{2,1,0:T(8,128)S(1)} %copy.48, f32[8,2,384,384]{3,2,1,0:T(8,128)} %get-tuple-element.147, s32[]{:T(128)S(6)} %copy.41, pred[]{:T(512)S(6)} %lt.40), kind=kOutput, calls=%fused_computation.clone.1 | convolution fusion | flops 1359249408 | bytes 4718597 | tf_op jit(solution)/shard_map/while/body/eval_jaxpr/kab,kbc->kac/dot_general | solution.py:22
  131.6 3.7 %convolution_select_fusion.2 = f32[2,384,384]{2,1,0:T(8,128)S(1)} fusion(f32[2,384,384]{2,1,0:T(8,128)S(1)} %copy.48, f32[8,2,384,384]{3,2,1,0:T(8,128)} %get-tuple-element.147, s32[]{:T(128)S(6)} %copy.41, pred[]{:T(512)S(6)} %lt.40), kind=kOutput, calls=%fused_computation.clone.1 | convolution fusion | flops 1359249408 | bytes 4718597 | tf_op jit(solution)/shard_map/while/body/eval_jaxpr/kab,kbc->kac/dot_general | solution.py:22
  135.3 2.5 %fusion.48 = f32[2,384,384]{2,1,0:T(8,128)S(1)} fusion(f32[2,384,384]{2,1,0:T(8,128)S(1)} %get-tuple-element.96, f32[2,384,384]{1,2,0:T(8,128)S(1)} %bitcast.74), kind=kOutput, calls=%fused_computation.49 | convolution fusion | flops 1358954496 | bytes 3538944 | tf_op jit(solution)/shard_map/while/body/eval_jaxpr/kab,kbc->kac/dot_general | solution.py:22
  137.8 2.5 %fusion.16 = f32[2,384,384]{2,1,0:T(8,128)S(1)} fusion(f32[2,384,384]{2,1,0:T(8,128)S(1)} %fusion.48, f32[2,384,384]{2,1,0:T(8,128)S(1)} %copy-done, f32[2,384,384]{1,2,0:T(8,128)S(1)} %copy-done.1), kind=kOutput, calls=%fused_computation.16 | convolution fusion | flops 1359544320 | bytes 4718592 | tf_op jit(solution)/shard_map/kab,ksbc->ksac/dot_general | solution.py:62
  140.4 2.6 %convolution_bitcast_fusion = f32[2,1,4,2,96,192]{4,5,2,3,0,1:T(8,128)S(1)} fusion(f32[2,384,2,192,1]{1,3,4,2,0:T(8,128)S(1)} %bitcast.77, f32[2,384,4,96,1]{1,3,2,4,0:T(8,128)S(1)} %bitcast.75), kind=kOutput, calls=%fused_computation.11 | convolution fusion | flops 1358954496 | bytes 3538944 | tf_op jit(solution)/shard_map/ksbir,ksbjq->ksijrq/dot_general | solution.py:70
  143.1 0.6 copy.21
  143.7 0.1 copy.22
  143.8 40.2 %all_to_all.25 = f32[2,1,8,96,192]{4,3,0,1,2:T(8,128)S(1)} all-to-all(f32[2,1,8,96,192]{4,3,0,1,2:T(8,128)S(1)} %copy.22), channel_id=1, replica_groups=mesh['drive'=2,'tm'=4,'mom'=2,'col'=2] {'tm','col'}, dimensions={2} | all-to-all | bytes 2359296 | tf_op jit(solution)/shard_map/all_to_all | solution.py:72
  184.0 2.4 %fusion.10 = f32[2,1,8,96,192]{4,2,3,0,1:T(8,128)S(1)} fusion(f32[2,1,8,96,192]{4,3,0,1,2:T(8,128)S(1)} %all_to_all.25), kind=kOutput, calls=%fused_computation.10 | convolution fusion | flops 28312576 | bytes 2359296 | tf_op jit(solution)/shard_map/ft,ktrc->kfrc/dot_general | solution.py:43
  186.4 2.5 %fusion.7 = f32[2,1,8,96,192]{4,2,3,0,1:T(8,128)S(1)} fusion(f32[2,1,8,96,192]{4,3,0,1,2:T(8,128)S(1)} %all_to_all.25), kind=kOutput, calls=%fused_computation.9 | convolution fusion | flops 28312512 | bytes 2359296 | tf_op jit(solution)/shard_map/ft,ktrc->kfrc/dot_general | solution.py:42
  188.9 0.2 pad_maximum_fusion
  189.1 2.6 %copy.24 = f32[2,2,8,96,192]{4,3,2,1,0:T(8,128)} copy(f32[2,2,8,96,192]{4,2,3,0,1:T(8,128)S(1)} %pad_maximum_fusion) | data formatting | bytes 4718592 | tf_op jit(solution)/shard_map/stack | solution.py:44
  (7 shorter events, 0.2 us)
Async XLA Ops:
  6.5 101.1 %all-gather.2.cloned.1.call-start = ((), (), s32[]{:S(2)}) async-start(), calls=%async_computation.2 | async-start | bytes 10616832 | tf_op jit(solution)/shard_map/all_gather | solution.py:11
  14.0 1.3 copy-start
  135.3 2.5 %copy-start.1 = (f32[2,384,384]{1,2,0:T(8,128)S(1)}, f32[2,384,384]{1,2,0:T(8,128)}, u32[]{:S(2)}) copy-start(f32[2,384,384]{1,2,0:T(8,128)} %copy.20) | copy-start | bytes 3538948
Sparse Core Ops, SparseCore 0:
  14.2 93.4 all-gather.1
where the time goes:
time: 199 us
  waiting for transfers between devices  90.1 us (45%)
  blocking collectives  44.9 us (23%)
  matrix products  38.2 us (19%)
  between operations  13.5 us (7%)
  local copies, waits for them, and re-layouts  10.5 us (5%)
    all_gather x1, waiting for transfers between devices, prefix_2(): pieces = lax.all_gather(value, axis)  90.1 us
    all_to_all x1, blocking collectives, body(): lax.all_to_all(heis, ('tm', 'col'), split_axis=2, concat_axis=1, tiled=True)  40.2 us
    dot_general x8, matrix products, multiply(): jnp.einsum('kab,kbc->kac', left, right, precision=lax.Precision.HIGHEST)  28.2 us
    all_to_all x1, blocking collectives, body(): lax.all_to_all(propagators, 'col', split_axis=1, concat_axis=3, tiled=True)  4.68 us
  transfers between devices with their start and end apart: 1, of which 1 were waited for; matrix products, arithmetic and copies ran while one was open for 1% of the time, Pallas kernels for 0%

commit v1 on v0

--- a/solution.py
+++ b/solution.py
@@ -3,7 +3,11 @@
 import jax
 import jax.numpy as jnp
 from jax import lax
+from jax.experimental import pallas as pl
+from jax.experimental.pallas import tpu as pltpu
 from jax.sharding import PartitionSpec as P
+
+CHUNKS = 3
 
 
 def prefix_2(value, axis, join, neutral):
@@ -44,11 +48,7 @@
     return jnp.stack([real, imag], axis=1)
 
 
-def owner_block(block):
-    return spectrum_block(block[:, :, 0])
-
-
-def body(propagators, current_op):
+def general_body(propagators, current_op):
     sym = 0.5 * (current_op + jnp.swapaxes(current_op, 1, 2))
     whole = lax.all_to_all(propagators, "col", split_axis=1, concat_axis=3, tiled=True)
     kdev = whole.shape[0]
@@ -69,10 +69,227 @@
     right = weighted.reshape(kdev, slices, order, n_cols, col_width)
     heis = jnp.einsum("ksbir,ksbjq->ksijrq", left, right, precision=lax.Precision.HIGHEST)
     heis = heis.reshape(kdev, slices, n_rows * n_cols, row_width, col_width)
-    return owner_block(lax.all_to_all(heis, ("tm", "col"), split_axis=2, concat_axis=1, tiled=True))
+    block = lax.all_to_all(heis, ("tm", "col"), split_axis=2, concat_axis=1, tiled=True)
+    return spectrum_block(block[:, :, 0])
+
+
+def halves(x):
+    high = x.astype(jnp.bfloat16)
+    return high, (x - high.astype(jnp.float32)).astype(jnp.bfloat16)
+
+
+def as_left(x):
+    high, low = halves(x)
+    return jnp.concatenate([high, high, low], axis=1)
+
+
+def as_right(x):
+    high, low = halves(x)
+    return jnp.concatenate([high, low, high], axis=0)
+
+
+def as_right_t(x):
+    high, low = halves(x)
+    return jnp.concatenate([high, low, high], axis=1)
+
+
+def product(left, right):
+    return jnp.dot(left, right, preferred_element_type=jnp.float32)
+
+
+def product_t(left, right):
+    dims = (((1,), (1,)), ((), ()))
+    return lax.dot_general(left, right, dims, preferred_element_type=jnp.float32)
+
+
+VMEM = pl.BlockSpec(memory_space=pltpu.VMEM)
+
+
+def local_call(kernel, outs, args, scratch=(), name=None):
+    return pl.pallas_call(
+        kernel,
+        out_shape=[jax.ShapeDtypeStruct(s, jnp.float32) for s in outs],
+        in_specs=[VMEM] * len(args),
+        out_specs=[VMEM] * len(outs),
+        scratch_shapes=list(scratch),
+        name=name,
+    )(*args)
+
+
+def start_kernel(mine_ref, got_ref, op_ref, a0_ref, a1_ref, sym_ref, *prod_refs):
+    core = lax.axis_index("col")
+    part = got_ref.shape[1]
+    for s, a_ref in enumerate((a0_ref, a1_ref)):
+        a_ref[pl.ds(pl.multiple_of(core * part, 8), part), :] = mine_ref[core, s]
+        a_ref[pl.ds(pl.multiple_of((1 - core) * part, 8), part), :] = got_ref[s]
+    right = as_right(a1_ref[...])
+    row = 0
+    for p_ref in prod_refs:
+        rows = p_ref.shape[0]
+        p_ref[...] = product(as_left(a0_ref[row:row + rows, :]), right)
+        row += rows
+    op = op_ref[core]
+    sym_ref[...] = 0.5 * (op + op.T)
+
+
+def hop_kernel(place, in_ref, *refs):
+    *prod_refs, out_ref = refs
+
+    @pl.when(lax.axis_index("tm") == place)
+    def _():
+        b = jnp.concatenate([r[...] for r in prod_refs], axis=0)
+        out_ref[...] = product(as_left(in_ref[...]), as_right(b))
+
+
+def heis_kernel(place, count, chunks, *refs):
+    ins, outs, (r_ref, s_ref) = refs[:2 + 2 * chunks], refs[2 + 2 * chunks:-2], refs[-2:]
+    a0_ref, sym_ref = ins[:2]
+    before, after = ins[2:2 + chunks], ins[2 + chunks:]
+
+    @pl.when(lax.axis_index("tm") == place)
+    def _():
+        order = a0_ref.shape[0]
+        rows = order // count
+        step = order // chunks
+        for q in range(chunks):
+            r_ref[0, q * step:(q + 1) * step, :] = before[q][...]
+            r_ref[2, q * step:(q + 1) * step, :] = after[q][...]
+        s_ref[...] = as_right(sym_ref[...])
+        if place == 0:
+            r_ref[1] = a0_ref[...]
+        else:
+            r_ref[1] = product(as_left(r_ref[0]), as_right(a0_ref[...]))
+        for i in ((1, 2) if place == 0 else (0, 1, 2)):
+            top = 0 if i >= 1 else place * rows
+            bottom = order if i <= 1 else (place + 1) * rows
+            weighted = product(as_left(r_ref[i, top:bottom, :]), s_ref[...])
+            heis = product_t(as_left(weighted), as_right_t(r_ref[i]))
+            for to in range(top // rows, bottom // rows):
+                first = (1 if place == 0 else 0) if to >= place else 1
+                outs[to][i - first] = heis[to * rows - top:(to + 1) * rows - top, :]
+
+
+def sent_slices(place, to):
+    first = max(2 * place - 1, 0) if to >= place else 2 * place
+    last = 2 * place if to > place else 2 * place + 1
+    return list(range(first, last + 1))
+
+
+def gather_kernel(count, *refs):
+    ins, (keep_ref, send_ref) = refs[:-2], refs[-2:]
+    core = lax.axis_index("col")
+    width = keep_ref.shape[2]
+    for to in range(count):
+        @pl.when(lax.axis_index("tm") == to)
+        def _(to=to):
+            for c in range(2):
+                @pl.when(core == c)
+                def _(c=c):
+                    for place in range(count):
+                        for i, t in enumerate(sent_slices(place, to)):
+                            block = ins[place * count + to][i]
+                            keep_ref[t] = block[:, c * width:(c + 1) * width]
+                            send_ref[t] = block[:, (1 - c) * width:(2 - c) * width]
+
+
+def spectrum_kernel(keep_ref, got_ref, out_ref):
+    core = lax.axis_index("col")
+    length, rows, width = keep_ref.shape
+    scale = 1.0 / math.sqrt(length)
+    step = 8
+
+    def cosine(n):
+        return scale * math.cos(2.0 * math.pi * (n % length) / length)
+
+    def sine(n):
+        return scale * math.sin(2.0 * math.pi * (n % length) / length)
+
+    def block(source, k, row):
+        here = pl.ds(pl.multiple_of(row * step, step), step)
+        values = [source[t, here, :] for t in range(length)]
+        for f in range(length // 2 + 1):
+            real = sum(cosine(f * t) * values[t] for t in range(length))
+            out_ref[k, 0, f, here, :] = real
+            mirrored = (length - f) % length
+            if mirrored != f:
+                imag = sum(-sine(f * t) * values[t] for t in range(1, length))
+                out_ref[k, 0, mirrored, here, :] = real
+                out_ref[k, 1, f, here, :] = imag
+                out_ref[k, 1, mirrored, here, :] = -imag
+            else:
+                imag = sum(-sine(f * t) * values[t] for t in range(length))
+                out_ref[k, 1, f, here, :] = imag
+
+    def turn(row, carry):
+        block(keep_ref, core, row)
+        block(got_ref, 1 - core, row)
+        return carry
+
+    lax.fori_loop(0, rows // step, turn, 0)
+
+
+def paired_body(propagators, current_op):
+    count = lax.axis_size("tm")
+    core = lax.axis_index("col")
+    flipped = jnp.swapaxes(propagators, 2, 3)
+    kdev, slices, part, order = flipped.shape
+    rows = order // count
+    swap = [(0, 1), (1, 0)]
+    other = lax.dynamic_index_in_dim(flipped, 1 - core, 0, keepdims=False)
+    got = lax.ppermute(other, "col", swap)
+    step = order // CHUNKS
+    square, chunk = (order, order), (step, order)
+    a0, a1, sym, *prod = local_call(
+        start_kernel, [square] * 3 + [chunk] * CHUNKS, (flipped, got, current_op), name="start"
+    )
+    moved = [[None] * count for _ in range(count)]
+
+    def send(place, to):
+        moved[place][to] = lax.ppermute(outs[place][to], "tm", [(place, to)])
+
+    outs = []
+    before, after = prod, prod
+    for place in range(count):
+        if place > 0:
+            before = [lax.ppermute(x, "tm", [(place - 1, place)]) for x in after]
+            after = [
+                local_call(lambda *r, p=place: hop_kernel(p, *r), [chunk], (x, *prod), name="hop")[0]
+                for x in before
+            ]
+        shapes = [(len(sent_slices(place, to)), rows, order) for to in range(count)]
+        outs.append(
+            local_call(
+                lambda *r, p=place: heis_kernel(p, count, CHUNKS, *r),
+                shapes,
+                (a0, sym, *before, *after),
+                scratch=[pltpu.VMEM((3, order, order), jnp.float32), pltpu.VMEM((3 * order, order), jnp.bfloat16)],
+                name="heis",
+            )
+        )
+        moved[place][place] = outs[place][place]
+        for to in range(count):
+            if to != place:
+                send(place, to)
+    pieces = [moved[place][to] for place in range(count) for to in range(count)]
+    width = order // 2
+    keep, give = local_call(
+        lambda *r: gather_kernel(count, *r), [(count * slices, rows, width)] * 2, pieces, name="gather"
+    )
+    taken = lax.ppermute(give, "col", swap)
+    return local_call(
+        spectrum_kernel, [(kdev, 2, count * slices, rows, width)], (keep, taken), name="spectrum"
+    )[0]
 
 
 def solution(mesh):
+    def body(propagators, current_op):
+        kdev, slices, order, _ = propagators.shape
+        count = mesh.shape["tm"]
+        paired = kdev == 2 and mesh.shape["col"] == 2 and slices == 2 and count > 1
+        if paired and order % (16 * CHUNKS) == 0 and order % (16 * count) == 0:
+            return paired_body(propagators, current_op)
+        return general_body(propagators, current_op)
+
     return jax.shard_map(
         body,
         mesh=mesh,

time: 199 us -> 103 us (0.52)
  the two profiles are of different devices: /device:TPU:0 before, /device:TPU:15 now
where the time goes in v1:
time: 103 us; the launch traced here: 102 us
  Pallas kernels  43.2 us (42%)
  waiting for transfers between devices  25.7 us (25%)
  starting transfers between devices  24.4 us (24%)
  local copies, waits for them, and re-layouts  7.93 us (8%)
    pallas_call x16, Pallas kernels, local_call(): pl.pallas_call(kernel, out_shape=[jax.ShapeDtypeStruct(s, jnp.float32) fo...  43.2 us
    ppermute x12, waiting for transfers between devices, send(): moved[place][to] = lax.ppermute(outs[place][to], 'tm', [(place, to)])  17.6 us
    ppermute x12, starting transfers between devices, send(): moved[place][to] = lax.ppermute(outs[place][to], 'tm', [(place, to)])  12 us
    ppermute x9, starting transfers between devices, paired_body(): before = [lax.ppermute(x, 'tm', [(place - 1, place)]) for x in after]  9.71 us
    unnamed x56, local copies, waits for them, and re-layouts  6.83 us
    ppermute x9, waiting for transfers between devices, paired_body(): before = [lax.ppermute(x, 'tm', [(place - 1, place)]) for x in after]  4.38 us
    ppermute x1, waiting for transfers between devices, paired_body(): taken = lax.ppermute(give, 'col', swap)  2.12 us
  transfers between devices with their start and end apart: 23, of which 5 were waited for; matrix products, arithmetic and copies ran while one was open for 0% of the time, Pallas kernels for 31%

profile of v1, /device:TPU:15, one launch (start us, length us, event | category | flops | bytes accessed | tf_op | source)
XLA Modules:
  0.0 101.7 jit_solution(2434683997787532508)
XLA Ops:
  1.8 1.6 %collective-permute-done.got_ref = f32[2,192,384]{2,1,0:T(8,128)S(1)} collective-permute-done((f32[2,192,384]{2,1,0:T(8,128)S(1)}, f32[2,192,384]{2,1,0:T(8,128)S(1)}, u32[]{:S(2)}, u32[]{:S(2)}) %collective-permute-start) | collective-permute-done | bytes 589856 | tf_op jit(solution)/shard_map/ppermute | solution.py:239
  4.3 3.5 %start.1 = (f32[384,384]{1,0:T(8,128)}, f32[384,384]{1,0:T(8,128)}, f32[384,384]{1,0:T(8,128)}, f32[128,384]{1,0:T(8,128)}, f32[128,384]{1,0:T(8,128)}, /*index=5*/f32[128,384]{1,0:T(8,128)}) custom-call(f32[2,2,192,384]{3,2,1,0:T(8,128)} %bitcast.5, f32[2,192,384]{2,1,0:T(8,128)} %copy-done.10, f32[2,384,384]{2,1,0:T(8,128)} %op_ref.1), custom_call_target="tpu_custom_call" | custom-call | tf_op jit(solution)/shard_map/start/pallas_call | solution.py:109
  7.8 1.3 %collective-permute-start.6 = (f32[128,384]{1,0:T(8,128)}, f32[128,384]{1,0:T(8,128)S(1)}, u32[]{:S(2)}, u32[]{:S(2)}) collective-permute-start(f32[128,384]{1,0:T(8,128)} %get-tuple-element.32.r_4_.r_7_.r_3_), channel_id=1, source_target_pairs={{0,4},{1,5},{2,6},{3,7},{16,20},{17,21},{18,22},{19,23}} | collective-permute-start | bytes 589832 | tf_op jit(solution)/shard_map/ppermute | solution.py:254
  9.1 1.3 %collective-permute-start.5 = (f32[128,384]{1,0:T(8,128)}, f32[128,384]{1,0:T(8,128)S(1)}, u32[]{:S(2)}, u32[]{:S(2)}) collective-permute-start(f32[128,384]{1,0:T(8,128)} %get-tuple-element.31.r_3_.r_6_.r_2_), channel_id=1, source_target_pairs={{0,4},{1,5},{2,6},{3,7},{16,20},{17,21},{18,22},{19,23}} | collective-permute-start | bytes 589832 | tf_op jit(solution)/shard_map/ppermute | solution.py:254
  10.4 1.3 %collective-permute-start.4 = (f32[128,384]{1,0:T(8,128)}, f32[128,384]{1,0:T(8,128)S(1)}, u32[]{:S(2)}, u32[]{:S(2)}) collective-permute-start(f32[128,384]{1,0:T(8,128)} %get-tuple-element.30.r_2_.r_5_.r_1_), channel_id=1, source_target_pairs={{0,4},{1,5},{2,6},{3,7},{16,20},{17,21},{18,22},{19,23}} | collective-permute-start | bytes 589832 | tf_op jit(solution)/shard_map/ppermute | solution.py:254
  11.7 4.3 %collective-permute-done.6.r_0_.r_4_ = f32[128,384]{1,0:T(8,128)S(1)} collective-permute-done((f32[128,384]{1,0:T(8,128)}, f32[128,384]{1,0:T(8,128)S(1)}, u32[]{:S(2)}, u32[]{:S(2)}) %collective-permute-start.6) | collective-permute-done | bytes 196640 | tf_op jit(solution)/shard_map/ppermute | solution.py:254
  16.7 2.2 %hop.11.r_7_ = f32[128,384]{1,0:T(8,128)} custom-call(f32[128,384]{1,0:T(8,128)} %copy-done.3, f32[128,384]{1,0:T(8,128)} %get-tuple-element.30.r_2_.r_5_.r_1_, f32[128,384]{1,0:T(8,128)} %get-tuple-element.31.r_3_.r_6_.r_2_, f32[128,384]{1,0:T(8,128)} %get-tuple-element.32.r_4_.r_7_.r_3_), custom_call_target="tpu_custom_call" | custom-call | tf_op jit(solution)/shard_map/hop/pallas_call | solution.py:109
  18.9 1.3 %collective-permute-start.12 = (f32[128,384]{1,0:T(8,128)}, f32[128,384]{1,0:T(8,128)S(1)}, u32[]{:S(2)}, u32[]{:S(2)}) collective-permute-start(f32[128,384]{1,0:T(8,128)} %hop.11.r_7_), channel_id=1, source_target_pairs={{4,8},{5,9},{6,10},{7,11},{20,24},{21,25},{22,26},{23,27}} | collective-permute-start | bytes 589832 | tf_op jit(solution)/shard_map/ppermute | solution.py:254
  20.9 2.2 %hop.10.r_6_ = f32[128,384]{1,0:T(8,128)} custom-call(f32[128,384]{1,0:T(8,128)} %copy-done.5, f32[128,384]{1,0:T(8,128)} %get-tuple-element.30.r_2_.r_5_.r_1_, f32[128,384]{1,0:T(8,128)} %get-tuple-element.31.r_3_.r_6_.r_2_, f32[128,384]{1,0:T(8,128)} %get-tuple-element.32.r_4_.r_7_.r_3_), custom_call_target="tpu_custom_call" | custom-call | tf_op jit(solution)/shard_map/hop/pallas_call | solution.py:109
  23.1 1.3 %collective-permute-start.11 = (f32[128,384]{1,0:T(8,128)}, f32[128,384]{1,0:T(8,128)S(1)}, u32[]{:S(2)}, u32[]{:S(2)}) collective-permute-start(f32[128,384]{1,0:T(8,128)} %hop.10.r_6_), channel_id=1, source_target_pairs={{4,8},{5,9},{6,10},{7,11},{20,24},{21,25},{22,26},{23,27}} | collective-permute-start | bytes 589832 | tf_op jit(solution)/shard_map/ppermute | solution.py:254
  25.1 2.2 %hop.9.r_5_ = f32[128,384]{1,0:T(8,128)} custom-call(f32[128,384]{1,0:T(8,128)} %copy-done.7, f32[128,384]{1,0:T(8,128)} %get-tuple-element.30.r_2_.r_5_.r_1_, f32[128,384]{1,0:T(8,128)} %get-tuple-element.31.r_3_.r_6_.r_2_, f32[128,384]{1,0:T(8,128)} %get-tuple-element.32.r_4_.r_7_.r_3_), custom_call_target="tpu_custom_call" | custom-call | tf_op jit(solution)/shard_map/hop/pallas_call | solution.py:109
  27.3 1.3 %collective-permute-start.10 = (f32[128,384]{1,0:T(8,128)}, f32[128,384]{1,0:T(8,128)S(1)}, u32[]{:S(2)}, u32[]{:S(2)}) collective-permute-start(f32[128,384]{1,0:T(8,128)} %hop.9.r_5_), channel_id=1, source_target_pairs={{4,8},{5,9},{6,10},{7,11},{20,24},{21,25},{22,26},{23,27}} | collective-permute-start | bytes 589832 | tf_op jit(solution)/shard_map/ppermute | solution.py:254
  29.3 1.9 %hop.14.r_7_ = f32[128,384]{1,0:T(8,128)} custom-call(f32[128,384]{1,0:T(8,128)} %copy-done.6, f32[128,384]{1,0:T(8,128)} %get-tuple-element.30.r_2_.r_5_.r_1_, f32[128,384]{1,0:T(8,128)} %get-tuple-element.31.r_3_.r_6_.r_2_, f32[128,384]{1,0:T(8,128)} %get-tuple-element.32.r_4_.r_7_.r_3_), custom_call_target="tpu_custom_call" | custom-call | tf_op jit(solution)/shard_map/hop/pallas_call | solution.py:109
  32.5 1.9 %hop.13.r_6_ = f32[128,384]{1,0:T(8,128)} custom-call(f32[128,384]{1,0:T(8,128)} %copy-done.8, f32[128,384]{1,0:T(8,128)} %get-tuple-element.30.r_2_.r_5_.r_1_, f32[128,384]{1,0:T(8,128)} %get-tuple-element.31.r_3_.r_6_.r_2_, f32[128,384]{1,0:T(8,128)} %get-tuple-element.32.r_4_.r_7_.r_3_), custom_call_target="tpu_custom_call" | custom-call | tf_op jit(solution)/shard_map/hop/pallas_call | solution.py:109
  35.1 2.6 %heis.4 = (f32[2,96,384]{2,1,0:T(8,128)}, f32[1,96,384]{2,1,0:T(8,128)}, f32[1,96,384]{2,1,0:T(8,128)}, f32[1,96,384]{2,1,0:T(8,128)}) custom-call(f32[384,384]{1,0:T(8,128)} %get-tuple-element.28.r_0_, f32[384,384]{1,0:T(8,128)} %get-tuple-element.29.r_1_, f32[128,384]{1,0:T(8,128)} %get-tuple-element.30.r_2_.r_5_.r_1_, ...), custom_call_target="tpu_custom_call" | custom-call | tf_op jit(solution)/shard_map/heis/pallas_call | solution.py:109
  37.7 1.3 %collective-permute-start.1 = (f32[1,96,384]{2,1,0:T(8,128)}, f32[1,96,384]{2,1,0:T(8,128)S(1)}, u32[]{:S(2)}, u32[]{:S(2)}) collective-permute-start(f32[1,96,384]{2,1,0:T(8,128)} %get-tuple-element.34), channel_id=1, source_target_pairs={{0,4},{1,5},{2,6},{3,7},{16,20},{17,21},{18,22},{19,23}} | collective-permute-start | bytes 442376 | tf_op jit(solution)/shard_map/ppermute | solution.py:248
  40.4 1.9 %hop.12.r_5_ = f32[128,384]{1,0:T(8,128)} custom-call(f32[128,384]{1,0:T(8,128)} %copy-done.9, f32[128,384]{1,0:T(8,128)} %get-tuple-element.30.r_2_.r_5_.r_1_, f32[128,384]{1,0:T(8,128)} %get-tuple-element.31.r_3_.r_6_.r_2_, f32[128,384]{1,0:T(8,128)} %get-tuple-element.32.r_4_.r_7_.r_3_), custom_call_target="tpu_custom_call" | custom-call | tf_op jit(solution)/shard_map/hop/pallas_call | solution.py:109
  43.0 5.8 %heis.5 = (f32[2,96,384]{2,1,0:T(8,128)}, f32[3,96,384]{2,1,0:T(8,128)}, f32[2,96,384]{2,1,0:T(8,128)}, f32[2,96,384]{2,1,0:T(8,128)}) custom-call(f32[384,384]{1,0:T(8,128)} %get-tuple-element.28.r_0_, f32[384,384]{1,0:T(8,128)} %get-tuple-element.29.r_1_, f32[128,384]{1,0:T(8,128)} %copy-done.7, f32[128,384]{1,0:T(8,128)} %copy-done.5, ...), custom_call_target="tpu_custom_call" | custom-call | tf_op jit(solution)/shard_map/heis/pallas_call | solution.py:109
  48.8 2.7 %heis.6 = (f32[2,96,384]{2,1,0:T(8,128)}, f32[2,96,384]{2,1,0:T(8,128)}, f32[3,96,384]{2,1,0:T(8,128)}, f32[2,96,384]{2,1,0:T(8,128)}) custom-call(f32[384,384]{1,0:T(8,128)} %get-tuple-element.28.r_0_, f32[384,384]{1,0:T(8,128)} %get-tuple-element.29.r_1_, f32[128,384]{1,0:T(8,128)} %copy-done.9, f32[128,384]{1,0:T(8,128)} %copy-done.8, ...), custom_call_target="tpu_custom_call" | custom-call | tf_op jit(solution)/shard_map/heis/pallas_call | solution.py:109
  51.5 1.5 %collective-permute-start.7 = (f32[2,96,384]{2,1,0:T(8,128)S(1)}, f32[2,96,384]{2,1,0:T(8,128)S(1)}, u32[]{:S(2)}, u32[]{:S(2)}) collective-permute-start(f32[2,96,384]{2,1,0:T(8,128)S(1)} %copy-done.26), channel_id=1, source_target_pairs={{4,0},{5,1},{6,2},{7,3},{20,16},{21,17},{22,18},{23,19}} | collective-permute-start | bytes 884744 | tf_op jit(solution)/shard_map/ppermute | solution.py:248
  53.1 1.3 %collective-permute-start.8 = (f32[2,96,384]{2,1,0:T(8,128)S(1)}, f32[2,96,384]{2,1,0:T(8,128)S(1)}, u32[]{:S(2)}, u32[]{:S(2)}) collective-permute-start(f32[2,96,384]{2,1,0:T(8,128)S(1)} %copy-done.25), channel_id=1, source_target_pairs={{4,8},{5,9},{6,10},{7,11},{20,24},{21,25},{22,26},{23,27}} | collective-permute-start | bytes 884744 | tf_op jit(solution)/shard_map/ppermute | solution.py:248
  54.4 1.3 %collective-permute-start.9 = (f32[2,96,384]{2,1,0:T(8,128)S(1)}, f32[2,96,384]{2,1,0:T(8,128)S(1)}, u32[]{:S(2)}, u32[]{:S(2)}) collective-permute-start(f32[2,96,384]{2,1,0:T(8,128)S(1)} %copy-done.24), channel_id=1, source_target_pairs={{4,12},{5,13},{6,14},{7,15},{20,28},{21,29},{22,30},{23,31}} | collective-permute-start | bytes 884744 | tf_op jit(solution)/shard_map/ppermute | solution.py:248
  57.2 1.9 %hop.17.r_7_ = f32[128,384]{1,0:T(8,128)} custom-call(f32[128,384]{1,0:T(8,128)} %copy-done.1, f32[128,384]{1,0:T(8,128)} %get-tuple-element.30.r_2_.r_5_.r_1_, f32[128,384]{1,0:T(8,128)} %get-tuple-element.31.r_3_.r_6_.r_2_, f32[128,384]{1,0:T(8,128)} %get-tuple-element.32.r_4_.r_7_.r_3_), custom_call_target="tpu_custom_call" | custom-call | tf_op jit(solution)/shard_map/hop/pallas_call | solution.py:109
  59.0 1.9 %hop.16.r_6_ = f32[128,384]{1,0:T(8,128)} custom-call(f32[128,384]{1,0:T(8,128)} %copy-done.2, f32[128,384]{1,0:T(8,128)} %get-tuple-element.30.r_2_.r_5_.r_1_, f32[128,384]{1,0:T(8,128)} %get-tuple-element.31.r_3_.r_6_.r_2_, f32[128,384]{1,0:T(8,128)} %get-tuple-element.32.r_4_.r_7_.r_3_), custom_call_target="tpu_custom_call" | custom-call | tf_op jit(solution)/shard_map/hop/pallas_call | solution.py:109
  60.9 1.9 %hop.15.r_5_ = f32[128,384]{1,0:T(8,128)} custom-call(f32[128,384]{1,0:T(8,128)} %copy-done.4, f32[128,384]{1,0:T(8,128)} %get-tuple-element.30.r_2_.r_5_.r_1_, f32[128,384]{1,0:T(8,128)} %get-tuple-element.31.r_3_.r_6_.r_2_, f32[128,384]{1,0:T(8,128)} %get-tuple-element.32.r_4_.r_7_.r_3_), custom_call_target="tpu_custom_call" | custom-call | tf_op jit(solution)/shard_map/hop/pallas_call | solution.py:109
  62.9 2.7 %heis.7 = (f32[2,96,384]{2,1,0:T(8,128)}, f32[2,96,384]{2,1,0:T(8,128)}, f32[2,96,384]{2,1,0:T(8,128)}, f32[3,96,384]{2,1,0:T(8,128)}) custom-call(f32[384,384]{1,0:T(8,128)} %get-tuple-element.28.r_0_, f32[384,384]{1,0:T(8,128)} %get-tuple-element.29.r_1_, f32[128,384]{1,0:T(8,128)} %copy-done.4, f32[128,384]{1,0:T(8,128)} %copy-done.2, ...), custom_call_target="tpu_custom_call" | custom-call | tf_op jit(solution)/shard_map/heis/pallas_call | solution.py:109
  65.6 1.3 %collective-permute-start.14 = (f32[2,96,384]{2,1,0:T(8,128)}, f32[2,96,384]{2,1,0:T(8,128)S(1)}, u32[]{:S(2)}, u32[]{:S(2)}) collective-permute-start(f32[2,96,384]{2,1,0:T(8,128)} %get-tuple-element.42), channel_id=1, source_target_pairs={{8,4},{9,5},{10,6},{11,7},{24,20},{25,21},{26,22},{27,23}} | collective-permute-start | bytes 884744 | tf_op jit(solution)/shard_map/ppermute | solution.py:248
  70.7 17.1 %collective-permute-done.14.r_9_ = f32[2,96,384]{2,1,0:T(8,128)S(1)} collective-permute-done((f32[2,96,384]{2,1,0:T(8,128)}, f32[2,96,384]{2,1,0:T(8,128)S(1)}, u32[]{:S(2)}, u32[]{:S(2)}) %collective-permute-start.14) | collective-permute-done | bytes 294944 | tf_op jit(solution)/shard_map/ppermute | solution.py:248
  89.0 3.8 %gather.1 = (f32[8,96,192]{2,1,0:T(8,128)}, f32[8,96,192]{2,1,0:T(8,128)}) custom-call(f32[2,96,384]{2,1,0:T(8,128)} %get-tuple-element.33.r_0_, f32[1,96,384]{2,1,0:T(8,128)} %copy-done.20, f32[1,96,384]{2,1,0:T(8,128)} %copy-done.21, f32[1,96,384]{2,1,0:T(8,128)} %copy-done.22, f32[2,96,384]{2,1,0:T(8,128)} %copy-done.11, ...), custom_call_target="tpu_custom_call" | custom-call | tf_op jit(solution)/shard_map/gather/pallas_call | solution.py:109
  92.8 1.9 %collective-permute-start.22 = (f32[8,96,192]{2,1,0:T(8,128)}, f32[8,96,192]{2,1,0:T(8,128)S(1)}, u32[]{:S(2)}, u32[]{:S(2)}) collective-permute-start(f32[8,96,192]{2,1,0:T(8,128)} %get-tuple-element.50), channel_id=1, source_target_pairs={{0,1},{1,0},{2,3},{3,2},{4,5},{5,4},{6,7},{7,6},{8,9},{9,8},{10,11... | collective-permute-start | bytes 1769480 | tf_op jit(solution)/shard_map/ppermute | solution.py:278
  94.7 2.1 %collective-permute-done.22.got_ref = f32[8,96,192]{2,1,0:T(8,128)S(1)} collective-permute-done((f32[8,96,192]{2,1,0:T(8,128)}, f32[8,96,192]{2,1,0:T(8,128)S(1)}, u32[]{:S(2)}, u32[]{:S(2)}) %collective-permute-start.22) | collective-permute-done | bytes 589856 | tf_op jit(solution)/shard_map/ppermute | solution.py:278
  97.7 4.1 %spectrum.1 = f32[2,2,8,96,192]{4,3,2,1,0:T(8,128)} custom-call(f32[8,96,192]{2,1,0:T(8,128)} %get-tuple-element.49.keep_ref, f32[8,96,192]{2,1,0:T(8,128)} %copy-done), custom_call_target="tpu_custom_call" | custom-call | tf_op jit(solution)/shard_map/spectrum/pallas_call | solution.py:109
  (87 shorter events, 16.5 us)
Async XLA Ops:
  1.1 2.4 %collective-permute-start = (f32[2,192,384]{2,1,0:T(8,128)S(1)}, f32[2,192,384]{2,1,0:T(8,128)S(1)}, u32[]{:S(2)}, u32[]{:S(2)}) collective-permute-start(f32[2,192,384]{2,1,0:T(8,128)S(1)} %dynamic-slice_bitcast_fusion), channel_id=1, source_target_pairs={{0,1},{1,0},{2,3},{3,2},{4,5},{5,4},{6,7},{7,6},{8,9},{9,8},{10,11... | collective-permute-start | bytes 1769480 | tf_op jit(solution)/shard_map/ppermute | solution.py:239
  7.8 8.2 %collective-permute-start.6 = (f32[128,384]{1,0:T(8,128)}, f32[128,384]{1,0:T(8,128)S(1)}, u32[]{:S(2)}, u32[]{:S(2)}) collective-permute-start(f32[128,384]{1,0:T(8,128)} %get-tuple-element.32.r_4_.r_7_.r_3_), channel_id=1, source_target_pairs={{0,4},{1,5},{2,6},{3,7},{16,20},{17,21},{18,22},{19,23}} | collective-permute-start | bytes 589832 | tf_op jit(solution)/shard_map/ppermute | solution.py:254
  9.1 11.1 %collective-permute-start.5 = (f32[128,384]{1,0:T(8,128)}, f32[128,384]{1,0:T(8,128)S(1)}, u32[]{:S(2)}, u32[]{:S(2)}) collective-permute-start(f32[128,384]{1,0:T(8,128)} %get-tuple-element.31.r_3_.r_6_.r_2_), channel_id=1, source_target_pairs={{0,4},{1,5},{2,6},{3,7},{16,20},{17,21},{18,22},{19,23}} | collective-permute-start | bytes 589832 | tf_op jit(solution)/shard_map/ppermute | solution.py:254
  10.4 14.0 %collective-permute-start.4 = (f32[128,384]{1,0:T(8,128)}, f32[128,384]{1,0:T(8,128)S(1)}, u32[]{:S(2)}, u32[]{:S(2)}) collective-permute-start(f32[128,384]{1,0:T(8,128)} %get-tuple-element.30.r_2_.r_5_.r_1_), channel_id=1, source_target_pairs={{0,4},{1,5},{2,6},{3,7},{16,20},{17,21},{18,22},{19,23}} | collective-permute-start | bytes 589832 | tf_op jit(solution)/shard_map/ppermute | solution.py:254
  18.9 9.7 %collective-permute-start.12 = (f32[128,384]{1,0:T(8,128)}, f32[128,384]{1,0:T(8,128)S(1)}, u32[]{:S(2)}, u32[]{:S(2)}) collective-permute-start(f32[128,384]{1,0:T(8,128)} %hop.11.r_7_), channel_id=1, source_target_pairs={{4,8},{5,9},{6,10},{7,11},{20,24},{21,25},{22,26},{23,27}} | collective-permute-start | bytes 589832 | tf_op jit(solution)/shard_map/ppermute | solution.py:254
  23.1 8.8 %collective-permute-start.11 = (f32[128,384]{1,0:T(8,128)}, f32[128,384]{1,0:T(8,128)S(1)}, u32[]{:S(2)}, u32[]{:S(2)}) collective-permute-start(f32[128,384]{1,0:T(8,128)} %hop.10.r_6_), channel_id=1, source_target_pairs={{4,8},{5,9},{6,10},{7,11},{20,24},{21,25},{22,26},{23,27}} | collective-permute-start | bytes 589832 | tf_op jit(solution)/shard_map/ppermute | solution.py:254
  27.3 12.4 %collective-permute-start.10 = (f32[128,384]{1,0:T(8,128)}, f32[128,384]{1,0:T(8,128)S(1)}, u32[]{:S(2)}, u32[]{:S(2)}) collective-permute-start(f32[128,384]{1,0:T(8,128)} %hop.9.r_5_), channel_id=1, source_target_pairs={{4,8},{5,9},{6,10},{7,11},{20,24},{21,25},{22,26},{23,27}} | collective-permute-start | bytes 589832 | tf_op jit(solution)/shard_map/ppermute | solution.py:254
  31.2 23.2 %collective-permute-start.18 = (f32[128,384]{1,0:T(8,128)}, f32[128,384]{1,0:T(8,128)S(1)}, u32[]{:S(2)}, u32[]{:S(2)}) collective-permute-start(f32[128,384]{1,0:T(8,128)} %hop.14.r_7_), channel_id=1, source_target_pairs={{8,12},{9,13},{10,14},{11,15},{24,28},{25,29},{26,30},{27,31}} | collective-permute-start | bytes 589832 | tf_op jit(solution)/shard_map/ppermute | solution.py:254
  34.5 21.3 %collective-permute-start.17 = (f32[128,384]{1,0:T(8,128)}, f32[128,384]{1,0:T(8,128)S(1)}, u32[]{:S(2)}, u32[]{:S(2)}) collective-permute-start(f32[128,384]{1,0:T(8,128)} %hop.13.r_6_), channel_id=1, source_target_pairs={{8,12},{9,13},{10,14},{11,15},{24,28},{25,29},{26,30},{27,31}} | collective-permute-start | bytes 589832 | tf_op jit(solution)/shard_map/ppermute | solution.py:254
  37.7 13.8 %collective-permute-start.1 = (f32[1,96,384]{2,1,0:T(8,128)}, f32[1,96,384]{2,1,0:T(8,128)S(1)}, u32[]{:S(2)}, u32[]{:S(2)}) collective-permute-start(f32[1,96,384]{2,1,0:T(8,128)} %get-tuple-element.34), channel_id=1, source_target_pairs={{0,4},{1,5},{2,6},{3,7},{16,20},{17,21},{18,22},{19,23}} | collective-permute-start | bytes 442376 | tf_op jit(solution)/shard_map/ppermute | solution.py:248
  39.0 14.0 %collective-permute-start.2 = (f32[1,96,384]{2,1,0:T(8,128)}, f32[1,96,384]{2,1,0:T(8,128)S(1)}, u32[]{:S(2)}, u32[]{:S(2)}) collective-permute-start(f32[1,96,384]{2,1,0:T(8,128)} %get-tuple-element.35), channel_id=1, source_target_pairs={{0,8},{1,9},{2,10},{3,11},{16,24},{17,25},{18,26},{19,27}} | collective-permute-start | bytes 442376 | tf_op jit(solution)/shard_map/ppermute | solution.py:248
  42.3 14.1 %collective-permute-start.16 = (f32[128,384]{1,0:T(8,128)}, f32[128,384]{1,0:T(8,128)S(1)}, u32[]{:S(2)}, u32[]{:S(2)}) collective-permute-start(f32[128,384]{1,0:T(8,128)} %hop.12.r_5_), channel_id=1, source_target_pairs={{8,12},{9,13},{10,14},{11,15},{24,28},{25,29},{26,30},{27,31}} | collective-permute-start | bytes 589832 | tf_op jit(solution)/shard_map/ppermute | solution.py:254
  48.7 5.7 %copy-start.24 = (f32[2,96,384]{2,1,0:T(8,128)S(1)}, f32[2,96,384]{2,1,0:T(8,128)}, u32[]{:S(2)}) copy-start(f32[2,96,384]{2,1,0:T(8,128)} %get-tuple-element.40) | copy-start | bytes 884740
  48.8 7.7 %copy-start.27 = (f32[1,96,384]{2,1,0:T(8,128)S(1)}, f32[1,96,384]{2,1,0:T(8,128)}, u32[]{:S(2)}) copy-start(f32[1,96,384]{2,1,0:T(8,128)} %get-tuple-element.36) | copy-start | bytes 442372
  51.5 36.4 %copy-start.20 = (f32[1,96,384]{2,1,0:T(8,128)}, f32[1,96,384]{2,1,0:T(8,128)S(1)}, u32[]{:S(2)}) copy-start(f32[1,96,384]{2,1,0:T(8,128)S(1)} %collective-permute-done.1.r_1_) | copy-start | bytes 442372
  51.5 15.3 %collective-permute-start.7 = (f32[2,96,384]{2,1,0:T(8,128)S(1)}, f32[2,96,384]{2,1,0:T(8,128)S(1)}, u32[]{:S(2)}, u32[]{:S(2)}) collective-permute-start(f32[2,96,384]{2,1,0:T(8,128)S(1)} %copy-done.26), channel_id=1, source_target_pairs={{4,0},{5,1},{6,2},{7,3},{20,16},{21,17},{22,18},{23,19}} | collective-permute-start | bytes 884744 | tf_op jit(solution)/shard_map/ppermute | solution.py:248
  53.0 34.9 %copy-start.21 = (f32[1,96,384]{2,1,0:T(8,128)}, f32[1,96,384]{2,1,0:T(8,128)S(1)}, u32[]{:S(2)}) copy-start(f32[1,96,384]{2,1,0:T(8,128)S(1)} %collective-permute-done.2.r_2_) | copy-start | bytes 442372
  53.1 14.5 %collective-permute-start.8 = (f32[2,96,384]{2,1,0:T(8,128)S(1)}, f32[2,96,384]{2,1,0:T(8,128)S(1)}, u32[]{:S(2)}, u32[]{:S(2)}) collective-permute-start(f32[2,96,384]{2,1,0:T(8,128)S(1)} %copy-done.25), channel_id=1, source_target_pairs={{4,8},{5,9},{6,10},{7,11},{20,24},{21,25},{22,26},{23,27}} | collective-permute-start | bytes 884744 | tf_op jit(solution)/shard_map/ppermute | solution.py:248
  54.4 14.3 %collective-permute-start.9 = (f32[2,96,384]{2,1,0:T(8,128)S(1)}, f32[2,96,384]{2,1,0:T(8,128)S(1)}, u32[]{:S(2)}, u32[]{:S(2)}) collective-permute-start(f32[2,96,384]{2,1,0:T(8,128)S(1)} %copy-done.24), channel_id=1, source_target_pairs={{4,12},{5,13},{6,14},{7,15},{20,28},{21,29},{22,30},{23,31}} | collective-permute-start | bytes 884744 | tf_op jit(solution)/shard_map/ppermute | solution.py:248
  55.7 14.3 %collective-permute-start.13 = (f32[2,96,384]{2,1,0:T(8,128)}, f32[2,96,384]{2,1,0:T(8,128)S(1)}, u32[]{:S(2)}, u32[]{:S(2)}) collective-permute-start(f32[2,96,384]{2,1,0:T(8,128)} %get-tuple-element.41), channel_id=1, source_target_pairs={{8,0},{9,1},{10,2},{11,3},{24,16},{25,17},{26,18},{27,19}} | collective-permute-start | bytes 884744 | tf_op jit(solution)/shard_map/ppermute | solution.py:248
  56.5 9.1 %collective-permute-start.3 = (f32[1,96,384]{2,1,0:T(8,128)S(1)}, f32[1,96,384]{2,1,0:T(8,128)S(1)}, u32[]{:S(2)}, u32[]{:S(2)}) collective-permute-start(f32[1,96,384]{2,1,0:T(8,128)S(1)} %copy-done.27), channel_id=1, source_target_pairs={{0,12},{1,13},{2,14},{3,15},{16,28},{17,29},{18,30},{19,31}} | collective-permute-start | bytes 442376 | tf_op jit(solution)/shard_map/ppermute | solution.py:248
  65.6 22.4 %copy-start.22 = (f32[1,96,384]{2,1,0:T(8,128)}, f32[1,96,384]{2,1,0:T(8,128)S(1)}, u32[]{:S(2)}) copy-start(f32[1,96,384]{2,1,0:T(8,128)S(1)} %collective-permute-done.3.r_3_) | copy-start | bytes 442372
  65.6 22.3 %collective-permute-start.14 = (f32[2,96,384]{2,1,0:T(8,128)}, f32[2,96,384]{2,1,0:T(8,128)S(1)}, u32[]{:S(2)}, u32[]{:S(2)}) collective-permute-start(f32[2,96,384]{2,1,0:T(8,128)} %get-tuple-element.42), channel_id=1, source_target_pairs={{8,4},{9,5},{10,6},{11,7},{24,20},{25,21},{26,22},{27,23}} | collective-permute-start | bytes 884744 | tf_op jit(solution)/shard_map/ppermute | solution.py:248
  66.9 21.1 %copy-start.11 = (f32[2,96,384]{2,1,0:T(8,128)}, f32[2,96,384]{2,1,0:T(8,128)S(1)}, u32[]{:S(2)}) copy-start(f32[2,96,384]{2,1,0:T(8,128)S(1)} %collective-permute-done.7.r_4_) | copy-start | bytes 884740
  66.9 20.9 %collective-permute-start.15 = (f32[2,96,384]{2,1,0:T(8,128)S(1)}, f32[2,96,384]{2,1,0:T(8,128)S(1)}, u32[]{:S(2)}, u32[]{:S(2)}) collective-permute-start(f32[2,96,384]{2,1,0:T(8,128)S(1)} %copy-done.23), channel_id=1, source_target_pairs={{8,12},{9,13},{10,14},{11,15},{24,28},{25,29},{26,30},{27,31}} | collective-permute-start | bytes 884744 | tf_op jit(solution)/shard_map/ppermute | solution.py:248
  67.6 20.4 %copy-start.12 = (f32[2,96,384]{2,1,0:T(8,128)}, f32[2,96,384]{2,1,0:T(8,128)S(1)}, u32[]{:S(2)}) copy-start(f32[2,96,384]{2,1,0:T(8,128)S(1)} %collective-permute-done.8.r_6_) | copy-start | bytes 884740
  67.6 20.2 %collective-permute-start.19 = (f32[2,96,384]{2,1,0:T(8,128)}, f32[2,96,384]{2,1,0:T(8,128)S(1)}, u32[]{:S(2)}, u32[]{:S(2)}) collective-permute-start(f32[2,96,384]{2,1,0:T(8,128)} %get-tuple-element.45), channel_id=1, source_target_pairs={{12,0},{13,1},{14,2},{15,3},{28,16},{29,17},{30,18},{31,19}} | collective-permute-start | bytes 884744 | tf_op jit(solution)/shard_map/ppermute | solution.py:248
  68.7 19.2 %copy-start.13 = (f32[2,96,384]{2,1,0:T(8,128)}, f32[2,96,384]{2,1,0:T(8,128)S(1)}, u32[]{:S(2)}) copy-start(f32[2,96,384]{2,1,0:T(8,128)S(1)} %collective-permute-done.9.r_7_) | copy-start | bytes 884740
  68.7 19.1 %collective-permute-start.20 = (f32[2,96,384]{2,1,0:T(8,128)}, f32[2,96,384]{2,1,0:T(8,128)S(1)}, u32[]{:S(2)}, u32[]{:S(2)}) collective-permute-start(f32[2,96,384]{2,1,0:T(8,128)} %get-tuple-element.46), channel_id=1, source_target_pairs={{12,4},{13,5},{14,6},{15,7},{28,20},{29,21},{30,22},{31,23}} | collective-permute-start | bytes 884744 | tf_op jit(solution)/shard_map/ppermute | solution.py:248
  70.0 18.0 %copy-start.14 = (f32[2,96,384]{2,1,0:T(8,128)}, f32[2,96,384]{2,1,0:T(8,128)S(1)}, u32[]{:S(2)}) copy-start(f32[2,96,384]{2,1,0:T(8,128)S(1)} %collective-permute-done.13.r_8_) | copy-start | bytes 884740
  70.0 17.9 %collective-permute-start.21 = (f32[2,96,384]{2,1,0:T(8,128)}, f32[2,96,384]{2,1,0:T(8,128)S(1)}, u32[]{:S(2)}, u32[]{:S(2)}) collective-permute-start(f32[2,96,384]{2,1,0:T(8,128)} %get-tuple-element.47), channel_id=1, source_target_pairs={{12,8},{13,9},{14,10},{15,11},{28,24},{29,25},{30,26},{31,27}} | collective-permute-start | bytes 884744 | tf_op jit(solution)/shard_map/ppermute | solution.py:248
  92.8 4.0 %collective-permute-start.22 = (f32[8,96,192]{2,1,0:T(8,128)}, f32[8,96,192]{2,1,0:T(8,128)S(1)}, u32[]{:S(2)}, u32[]{:S(2)}) collective-permute-start(f32[8,96,192]{2,1,0:T(8,128)} %get-tuple-element.50), channel_id=1, source_target_pairs={{0,1},{1,0},{2,3},{3,2},{4,5},{5,4},{6,7},{7,6},{8,9},{9,8},{10,11... | collective-permute-start | bytes 1769480 | tf_op jit(solution)/shard_map/ppermute | solution.py:278
  (19 other events, 32.0 us)
